TPU v7x, 512 devices: a whole 4x4x16 slice. The times are simulated.
512 devices in a mesh: dp: 16 (over x_lo, y, core), vocab: 32 (over z, x_hi).
Axes of the slice: x: 4 (x_hi: 2, x_lo: 2; x = x_hi * 2 + x_lo), y: 4, z: 16, core: 2. Of those that a mesh axis runs over, the one named last changes fastest.
Arguments:
- passage_hidden: bfloat16 [2048, 2048], P('dp'), may hold values from -7 to 7
- passage_lengths: int32 [32], P('dp'), may hold values from 16 to 64, as said below
- query_ids: int32 [32, 16], P('dp'), may hold values from 0 to 131071
- query_lengths: int32 [32], P('dp'), may hold values from 4 to 16, as said below
- positives: int32 [32], replicated, may hold values from 0 to 31, each once
- head: bfloat16 [2048, 131072], P('dp', 'vocab'), may hold values from -0.125 to 0.125
- df_prev: float32 [131072], P('vocab'), may hold values from 1 to 4096
Outputs:
- head_grad: float32 [2048, 131072], P('dp', 'vocab')
- scores: float32 [32, 32], replicated
Inputs may be any that keep to these rules, and one draw needn't show every extreme that they name: `passage_lengths`: some passage fills all 64 slots. `query_lengths`: some query fills all 16 slots. `positives`: each passage is the positive of exactly one query.
All inputs are finite; a program needn't handle non-finite values.
Results may differ from a plain program's by a relative error of at most 0.00064.
Values may be sent and summed in bfloat16 or wider, within the bound.
No kernel may reach another device: no remote copies, remote signals or barrier semaphores. Data moves between devices by JAX's collectives and lax.ppermute only.
A program may use at most 64 MiB of HBM per device.

v0:
```python
import jax
import jax.numpy as jnp
from jax import lax
from jax.sharding import PartitionSpec as P

flops_weight = 0.3


def ranking_grad(scores, chosen, query_total):
    columns = scores.shape[1]
    onehot = (jnp.arange(columns, dtype=jnp.int32)[None, :] == chosen[:, None]).astype(jnp.float32)
    own_score = jnp.sum(scores * onehot, axis=1, keepdims=True)
    sigmas = jax.nn.sigmoid(scores - own_score)
    return (sigmas - onehot * jnp.sum(sigmas, axis=1, keepdims=True)) / query_total


def local(passage_hidden, passage_lengths, query_ids, query_lengths, positives, head, df_prev):
    dp_count = lax.axis_size("dp")
    dp_index = lax.axis_index("dp")
    vocab_index = lax.axis_index("vocab")
    width_local = head.shape[1]
    column_count = width_local // dp_count
    head_block = lax.all_to_all(head, "dp", split_axis=1, concat_axis=0, tiled=True)
    hidden_all, passage_sizes, query_tokens, query_sizes = (
        lax.all_gather(passage_hidden, "dp", axis=0, tiled=True),
        lax.all_gather(passage_lengths, "dp", axis=0, tiled=True),
        lax.all_gather(query_ids, "dp", axis=0, tiled=True),
        lax.all_gather(query_lengths, "dp", axis=0, tiled=True),
    )
    passage_count = passage_sizes.shape[0]
    seq_span = hidden_all.shape[0] // passage_count
    logits = jnp.dot(hidden_all, head_block, preferred_element_type=jnp.float32)
    softened = jax.nn.softplus(logits)
    activation = jnp.log1p(softened)
    slope_term = jax.nn.sigmoid(logits) / (1.0 + softened)
    positions = jnp.arange(seq_span, dtype=jnp.int32)
    token_mask = (positions[None, :] < passage_sizes[:, None]).astype(jnp.float32)
    token_weight = token_mask / passage_sizes.astype(jnp.float32)[:, None]
    passage_rep = jnp.sum(
        activation.reshape(passage_count, seq_span, column_count) * token_weight[:, :, None], axis=1
    )
    first_column = dp_index * column_count
    doc_freq = lax.dynamic_slice_in_dim(df_prev, first_column, column_count, 0) + jnp.sum(
        1.0 - jnp.exp(-2.0 * passage_rep), axis=0
    )
    term_weight = jnp.log1p(doc_freq)
    column_ids = (
        vocab_index * width_local + first_column + jnp.arange(column_count, dtype=jnp.int32)
    )
    query_mask = jnp.arange(query_tokens.shape[1], dtype=jnp.int32)[None, :] < query_sizes[:, None]
    matches = (query_tokens[:, :, None] == column_ids[None, None, :]) & query_mask[:, :, None]
    query_bag = jnp.sum(matches.astype(jnp.float32), axis=1)
    partial_scores = jnp.dot(
        query_bag,
        passage_rep.T,
        precision=lax.Precision.HIGHEST,
        preferred_element_type=jnp.float32,
    )
    query_total = positives.shape[0]
    scores = lax.psum(partial_scores, ("dp", "vocab"))
    score_grad = ranking_grad(scores, positives, query_total)
    rep_grad = jnp.dot(
        score_grad.T, query_bag, precision=lax.Precision.HIGHEST, preferred_element_type=jnp.float32
    )
    rep_grad = rep_grad + 2.0 * flops_weight / passage_count * term_weight * jnp.mean(
        passage_rep, axis=0
    )
    logit_grad = (
        (token_weight[:, :, None] * rep_grad[:, None, :]).reshape(logits.shape) * slope_term
    ).astype(jnp.bfloat16)
    grad_block = lax.dot_general(
        hidden_all, logit_grad, (((0,), (0,)), ((), ())), preferred_element_type=jnp.float32
    )
    head_grad = lax.all_to_all(grad_block, "dp", split_axis=0, concat_axis=1, tiled=True)
    return (head_grad, scores)


def solution(mesh):
    return jax.shard_map(
        local,
        mesh=mesh,
        in_specs=(
            P("dp", None),
            P("dp"),
            P("dp", None),
            P("dp"),
            P(),
            P("dp", "vocab"),
            P("vocab"),
        ),
        out_specs=(P("dp", "vocab"), P()),
        check_vma=False,
    )
```

profile of v0, /device:TPU:1, one launch (start us, length us, event | category | flops | bytes accessed | tf_op | source)
XLA Modules:
  0.0 239.4 jit_solution(17797994850727579767)
XLA Ops:
  7.2 0.0 all-gather.3.cloned.1.call-start
  7.2 0.7 all-gather.3.cloned.1.call-update
  7.9 2.3 copy.18
  10.2 10.3 %all-to-all-start = ((bf16[128,16,256]{0,2,1:T(8,128)(2,1)}), bf16[128,16,256]{0,2,1:T(8,128)(2,1)S(1)}, u32[]{:S(2)}, u32[]{:S(2)}) async-start(bf16[128,16,256]{0,2,1:T(8,128)(2,1)} %bitcast.3), calls=%async_computation | async-start | bytes 2097152 | tf_op jit(solution)/shard_map/all_to_all | solution.py:23
  20.5 1.3 dynamic-slice
  22.4 0.2 dynamic-update-slice
  22.7 0.2 dynamic-update-slice.1
  22.9 18.3 %all-reduce.2 = (s32[32]{0:T(128)S(1)}, s32[32]{0:T(128)S(1)}) all-reduce(s32[32]{0:T(128)S(1)} %dynamic-update-slice.1, s32[32]{0:T(128)S(1)} %dynamic-update-slice), channel_id=1, replica_groups=mesh['dp'=16,'vocab'=32] {'dp'}, use_global_device_ids=true, to_apply=%add.1 | all-reduce | flops 64 | bytes 512
  41.2 0.1 convert_divide_fusion
  41.3 0.1 div.37
  41.4 0.0 copy-done.1
  41.4 19.2 %all-gather = s32[16,2,16]{2,1,0:T(2,128)S(1)} all-gather(s32[1,2,16]{2,1,0:T(2,128)S(1)} %bitcast.35), channel_id=1, replica_groups=mesh['dp'=16,'vocab'=32] {'dp'}, dimensions={0}, use_global_device_ids=true | all-gather | bytes 2176 | tf_op jit(solution)/shard_map/all_gather | solution.py:27
  60.6 0.1 iota_compare_fusion.2
  60.7 0.3 convert_reduce_fusion
  60.9 0.0 all-to-all-done
  61.0 0.5 copy.19
  61.5 15.2 %all-gather.3.cloned.1.call-done = bf16[2048,2048]{1,0:T(8,128)(2,1)} async-done(((bf16[128,2048]{1,0:T(8,128)(2,1)}), bf16[2048,2048]{1,0:T(8,128)(2,1)}) %all-gather.3.cloned.1.call-update) | async-done | bytes 8388624 | tf_op jit(solution)/shard_map/all_gather | solution.py:25
  76.7 7.4 %multiply_reduce_fusion = (f32[256]{0:T(256)S(1)}, f32[2048,256]{1,0:T(8,128)S(1)}) fusion(f32[2048]{0:T(1024)S(1)} %div.37, bf16[2048,2048]{1,0:T(8,128)(2,1)} %all-gather.3.cloned.1.call-done, bf16[2048,256]{1,0:T(8,128)(2,1)S(1)} %bitcast.33), kind=kOutput, calls=%fused_computation.5 | convolution fusion | flops 2151677696 | bytes 11543552 | tf_op jit(solution)/shard_map/dot_general | solution.py:32
  84.1 0.0 copy-start.2
  84.1 1.9 multiply_reduce_fusion.1
  86.1 0.2 fusion.13
  86.2 105.4 %psum.7 = f32[32,32]{1,0:T(8,128)S(1)} all-reduce(f32[32,32]{1,0:T(8,128)S(1)} %fusion.13), channel_id=1, replica_groups=mesh['dp'=16,'vocab'=32] {'dp','vocab'}, use_global_device_ids=true, to_apply=%region_2.3 | all-reduce | flops 1024 | bytes 8192 | tf_op jit(solution)/shard_map/psum | solution.py:60
  191.6 0.2 select_reduce_fusion
  191.8 0.2 fusion.12
  192.0 0.8 multiply_multiply_fusion
  192.8 0.3 convolution_add_fusion
  193.1 1.7 fusion.1
  194.9 5.7 %convolution_bitcast_fusion = f32[32,16,8,128]{3,2,1,0:T(8,128)S(1)} fusion(bf16[2048,256]{1,0:T(8,128)(2,1)S(1)} %fusion.1, bf16[2048,2048]{1,0:T(8,128)(2,1)} %all-gather.3.cloned.1.call-done), kind=kOutput, calls=%fused_computation.8 | convolution fusion | flops 2147483648 | bytes 11534336 | tf_op jit(solution)/shard_map/dot_general | solution.py:71
  200.6 0.0 copy-done
  200.6 0.2 copy.24
  200.8 30.0 %all_to_all.38 = f32[16,128,256]{1,2,0:T(8,128)S(1)} all-to-all(f32[16,128,256]{1,2,0:T(8,128)S(1)} %bitcast.30), channel_id=1, replica_groups=mesh['dp'=16,'vocab'=32] {'dp'}, dimensions={0} | all-to-all | bytes 4194304 | tf_op jit(solution)/shard_map/all_to_all | solution.py:74
  230.8 1.8 copy.21
  (12 shorter events, 0.1 us)
Async XLA Ops:
  7.2 69.5 %all-gather.3.cloned.1.call-start = ((), (), s32[]{:S(2)}) async-start(), calls=%async_computation.2 | async-start | bytes 8912896 | tf_op jit(solution)/shard_map/all_gather | solution.py:25
  7.9 14.5 %copy-start.3 = (s32[2]{0:T(128)S(1)}, s32[2]{0:T(128)}, u32[]{:S(2)}) copy-start(s32[2]{0:T(128)} %param.8) | copy-start | bytes 28
  7.9 14.8 %copy-start.4 = (s32[2]{0:T(128)S(1)}, s32[2]{0:T(128)}, u32[]{:S(2)}) copy-start(s32[2]{0:T(128)} %param.10) | copy-start | bytes 28
  7.9 33.5 %copy-start.1 = (s32[2,16]{1,0:T(2,128)S(1)}, s32[2,16]{1,0:T(2,128)}, u32[]{:S(2)}) copy-start(s32[2,16]{1,0:T(2,128)} %param.9) | copy-start | bytes 388
  10.2 50.7 %all-to-all-start = ((bf16[128,16,256]{0,2,1:T(8,128)(2,1)}), bf16[128,16,256]{0,2,1:T(8,128)(2,1)S(1)}, u32[]{:S(2)}, u32[]{:S(2)}) async-start(bf16[128,16,256]{0,2,1:T(8,128)(2,1)} %bitcast.3), calls=%async_computation | async-start | bytes 2097152 | tf_op jit(solution)/shard_map/all_to_all | solution.py:23
  84.1 107.6 %copy-start.2 = (s32[32]{0:T(128)S(1)}, s32[32]{0:T(128)}, u32[]{:S(2)}) copy-start(s32[32]{0:T(128)} %param.11) | copy-start | bytes 388
  191.6 9.0 %copy-start = (f32[32,32]{1,0:T(8,128)}, f32[32,32]{1,0:T(8,128)S(1)}, u32[]{:S(2)}) copy-start(f32[32,32]{1,0:T(8,128)S(1)} %psum.7) | copy-start | bytes 12292
Sparse Core Ops, SparseCore 0:
  10.1 66.5 all-gather.2
where the time goes:
time: 240 us; the launch traced here: 239 us
  blocking collectives  173 us (72%)
  waiting for transfers between devices  15.9 us (7%)
  between operations  14.8 us (6%)
  matrix products  13.6 us (6%)
  starting transfers between devices  10.3 us (4%)
  local copies, waits for them, and re-layouts  6.64 us (3%)
  other arithmetic  5.26 us (2%)
    psum x1, blocking collectives, local(): scores = lax.psum(partial_scores, ('dp', 'vocab'))  105 us
    all_to_all x1, blocking collectives, local(): lax.all_to_all(grad_block, 'dp', split_axis=0, concat_axis=1, tiled=True)  30 us
    all_gather x1, blocking collectives, local(): lax.all_gather(query_ids, 'dp', axis=0, tiled=True)  19.2 us
    unnamed x1, blocking collectives  18.3 us
    all_gather x1, waiting for transfers between devices, local(): lax.all_gather(passage_hidden, 'dp', axis=0, tiled=True)  15.2 us
    all_to_all x1, starting transfers between devices, local(): lax.all_to_all(head, 'dp', split_axis=1, concat_axis=0, tiled=True)  10.3 us
    dot_general x1, matrix products, local(): logits = jnp.dot(hidden_all, head_block, preferred_element_type=jnp.float32)  7.39 us
    unnamed x17, local copies, waits for them, and re-layouts  5.83 us
  transfers between devices with their start and end apart: 2, of which 1 were waited for; matrix products, arithmetic and copies ran while one was open for 2% of the time, Pallas kernels for 0%

commit v1 on v0

--- a/solution.py
+++ b/solution.py
@@ -57,7 +57,7 @@
         preferred_element_type=jnp.float32,
     )
     query_total = positives.shape[0]
-    scores = lax.psum(partial_scores, ("dp", "vocab"))
+    scores = jnp.sum(lax.all_gather(partial_scores, ("dp", "vocab")), axis=0)
     score_grad = ranking_grad(scores, positives, query_total)
     rep_grad = jnp.dot(
         score_grad.T, query_bag, precision=lax.Precision.HIGHEST, preferred_element_type=jnp.float32

time: 240 us -> 1580 us (6.58)
  waiting for transfers between devices: 15.9 us -> 1450 us
  blocking collectives: 173 us -> 67 us
    all_gather x0 -> x1, waiting for transfers between devices: none -> 1430 us  [local(): scores = jnp.sum(lax.all_gather(partial_scores, ('dp', 'vocab')), axis=0)]
    psum x1 -> x0, blocking collectives: 105 us -> none  [local(): scores = lax.psum(partial_scores, ('dp', 'vocab'))]
  transfers between devices with their start and end apart: 2 -> 3, of which waited for: 1 -> 2; matrix products, arithmetic and copies ran while one was open for 2% -> 0% of each run, Pallas kernels for 0% -> 0%
where the time goes in v1:
time: 1580 us; the launch traced here: 1570 us
  waiting for transfers between devices  1450 us (92%)
  blocking collectives  67 us (4%)
    all_gather x1, waiting for transfers between devices, local(): scores = jnp.sum(lax.all_gather(partial_scores, ('dp', 'vocab')), axis=0)  1430 us
  transfers between devices with their start and end apart: 3, of which 2 were waited for; matrix products, arithmetic and copies ran while one was open for 0% of the time, Pallas kernels for 0%

profile of v1, /device:TPU:1, one launch (start us, length us, event | category | flops | bytes accessed | tf_op | source)
XLA Modules:
  0.0 1570.6 jit_solution(8109224878212356220)
XLA Ops:
  7.2 0.0 all-gather.5.cloned.1.call-start
  7.2 0.7 all-gather.5.cloned.1.call-update
  7.9 2.3 copy.18
  10.2 10.3 all-to-all-start
  20.5 0.0 all-gather.7.cloned.1.call-start
  20.5 1.3 dynamic-slice
  22.5 0.2 dynamic-update-slice.1
  22.7 0.2 dynamic-update-slice
  22.9 18.3 %all-reduce.2 = (s32[32]{0:T(128)S(1)}, s32[32]{0:T(128)S(1)}) all-reduce(s32[32]{0:T(128)S(1)} %dynamic-update-slice.1, s32[32]{0:T(128)S(1)} %dynamic-update-slice), channel_id=1, replica_groups=mesh['dp'=16,'vocab'=32] {'dp'}, use_global_device_ids=true, to_apply=%add.1 | all-reduce | flops 64 | bytes 512
  41.2 0.1 convert_divide_fusion
  41.3 0.1 div.37
  41.4 19.2 %all-gather.1 = s32[16,2,16]{2,1,0:T(2,128)S(1)} all-gather(s32[1,2,16]{2,1,0:T(2,128)S(1)} %bitcast.37), channel_id=1, replica_groups=mesh['dp'=16,'vocab'=32] {'dp'}, dimensions={0}, use_global_device_ids=true | all-gather | bytes 2176 | tf_op jit(solution)/shard_map/all_gather | solution.py:27
  60.6 0.1 iota_compare_fusion.2
  60.7 0.3 convert_reduce_fusion
  61.0 0.5 copy.19
  61.5 15.2 all-gather.5.cloned.1.call-done
  76.7 7.4 multiply_reduce_fusion
  84.1 1.9 multiply_reduce_fusion.1
  86.0 0.8 fusion.13
  86.8 0.0 all-gather.7.cloned.1.call-update
  86.9 0.8 multiply_multiply_fusion
  87.6 1432.4 %all-gather.7.cloned.1.call-done = f32[16384,32]{1,0:T(8,128)} async-done(((f32[32,32]{1,0:T(8,128)}), f32[16384,32]{1,0:T(8,128)}) %all-gather.7.cloned.1.call-update) | async-done | bytes 2097168 | tf_op jit(solution)/shard_map/all_gather | solution.py:60
  1520.0 4.0 reduce_sum.65
  1524.1 0.0 copy-start
  1524.1 0.2 select_reduce_fusion
  1524.2 0.2 fusion.12
  1524.4 0.3 convolution_add_fusion
  1524.8 1.7 fusion.1
  1526.5 5.7 convolution_bitcast_fusion
  1532.3 0.2 copy.24
  1532.5 29.5 %all_to_all.38 = f32[16,128,256]{1,2,0:T(8,128)S(1)} all-to-all(f32[16,128,256]{1,2,0:T(8,128)S(1)} %bitcast.32), channel_id=1, replica_groups=mesh['dp'=16,'vocab'=32] {'dp'}, dimensions={0} | all-to-all | bytes 4194304 | tf_op jit(solution)/shard_map/all_to_all | solution.py:74
  1562.0 1.8 copy.21
  (15 shorter events, 0.1 us)
Async XLA Ops:
  7.2 69.5 %all-gather.5.cloned.1.call-start = ((), (), s32[]{:S(2)}) async-start(), calls=%async_computation.2 | async-start | bytes 8912896 | tf_op jit(solution)/shard_map/all_gather | solution.py:25
  7.9 14.6 copy-start.3
  7.9 14.8 copy-start.4
  7.9 33.5 %copy-start.1 = (s32[2,16]{1,0:T(2,128)S(1)}, s32[2,16]{1,0:T(2,128)}, u32[]{:S(2)}) copy-start(s32[2,16]{1,0:T(2,128)} %param.9) | copy-start | bytes 388
  10.2 50.7 %all-to-all-start = ((bf16[128,16,256]{0,2,1:T(8,128)(2,1)}), bf16[128,16,256]{0,2,1:T(8,128)(2,1)S(1)}, u32[]{:S(2)}, u32[]{:S(2)}) async-start(bf16[128,16,256]{0,2,1:T(8,128)(2,1)} %bitcast.3), calls=%async_computation | async-start | bytes 2097152 | tf_op jit(solution)/shard_map/all_to_all | solution.py:23
  20.5 1499.6 %all-gather.7.cloned.1.call-start = ((), (), s32[]{:S(2)}) async-start(), calls=%async_computation.3 | async-start | bytes 8404992 | tf_op jit(solution)/shard_map/all_gather | solution.py:60
  1520.0 4.0 copy-start.2
  1524.1 8.2 copy-start
Sparse Core Ops, SparseCore 0:
  10.1 66.5 all-gather.4
  86.9 1433.0 all-gather.6
